TPU v7x, 512 devices: a whole 4x4x16 slice. The times are simulated.
512 devices in a mesh: row: 16 (over y, x), col: 32 (over z, core).
Axes of the slice: x: 4, y: 4, z: 16, core: 2. Of those that a mesh axis runs over, the one named last changes fastest.
Arguments:
- panel: bfloat16 [4, 16, 512, 512], P(None, 'row', 'col'), may hold values from -1.1953125 to 1.1953125
- inverse_factor: bfloat16 [512, 512], replicated
- slot_rows: int32 [16, 32, 2], P('row', 'col'), may hold values from 0 to 63, as said below
- slot_cols: int32 [16, 32, 2], P('row', 'col'), may hold values from 0 to 63, as said below
- live_count: int32 [16, 32], P('row', 'col'), may hold values from 0 to 2
Outputs:
- contrib: bfloat16 [16, 32, 2, 512, 512], P('row', 'col')
Inputs may be any that keep to these rules, and one draw needn't show every extreme that they name: slot_rows[r, c, s] is congruent to r modulo 16; for s < live_count[r, c] the slots of one position name distinct blocks with slot_rows >= slot_cols; the other slots are ignored. slot_cols[r, c, s] is congruent to c modulo 32.
All inputs are finite; a program needn't handle non-finite values.
Results may differ from a plain program's by a relative error of at most 0.0054.
Values may be sent and summed in bfloat16 or wider, within the bound.
No kernel may reach another device: no remote copies, remote signals or barrier semaphores. Data moves between devices by JAX's collectives and lax.ppermute only.
A program may use at most 64 MiB of HBM per device.

v0:
```python
import jax
import jax.numpy as jnp
from jax import lax
from jax.sharding import PartitionSpec as P


def broadcast(value, axis, source):
    kept = jnp.where(lax.axis_index(axis) == source, value, 0).astype(value.dtype)
    return lax.psum(kept, axis)


def body(panel, inverse_factor, slot_rows, slot_cols, live_count):
    panel_count, _, part_rows, tile_width = panel.shape
    grid_rows = lax.axis_size("row")
    grid_cols = lax.axis_size("col")
    col_ratio = grid_cols // grid_rows
    column_count = panel_count // col_ratio
    solved = jnp.dot(
        panel.reshape(-1, tile_width), inverse_factor, preferred_element_type=jnp.float32
    )
    solved = solved.astype(jnp.bfloat16).reshape(panel_count, 1, part_rows, tile_width)
    row_blocks = lax.all_gather(solved, "col", axis=2, tiled=True).reshape(
        panel_count, tile_width, tile_width
    )
    position = lax.axis_index("col")
    grouped = row_blocks.reshape(column_count, col_ratio, tile_width, tile_width)
    picked = lax.dynamic_index_in_dim(grouped, position // grid_rows, 1, keepdims=False)
    col_blocks = broadcast(picked, "row", position % grid_rows)
    slot_total = slot_rows.shape[-1]
    rows_here = slot_rows.reshape(-1)
    cols_here = slot_cols.reshape(-1)
    live_here = live_count.reshape(())
    result = jnp.zeros((slot_total, tile_width, tile_width), jnp.bfloat16)

    def update(slot, current):
        left_tile = lax.dynamic_index_in_dim(
            row_blocks, rows_here[slot] // grid_rows, 0, keepdims=False
        )
        right_tile = lax.dynamic_index_in_dim(
            col_blocks, cols_here[slot] // grid_cols, 0, keepdims=False
        )
        product = lax.dot_general(
            left_tile, right_tile, (((1,), (1,)), ((), ())), preferred_element_type=jnp.float32
        )
        return lax.dynamic_update_index_in_dim(current, (-product).astype(jnp.bfloat16), slot, 0)

    result = lax.fori_loop(0, live_here, update, result)
    return result.reshape(1, 1, slot_total, tile_width, tile_width)


def solution(mesh):
    placed = (
        P(None, "row", "col", None),
        P(),
        P("row", "col", None),
        P("row", "col", None),
        P("row", "col"),
    )
    return jax.shard_map(
        body,
        mesh=mesh,
        in_specs=placed,
        out_specs=P("row", "col", None, None, None),
        check_vma=False,
    )
```

profile of v0, /device:TPU:32, one launch (start us, length us, event | category | flops | bytes accessed | tf_op | source)
XLA Modules:
  0.0 229.6 jit_solution(7024908279362446910)
XLA Ops:
  6.5 0.0 copy-start
  6.5 0.0 all-gather.2.cloned.1.call-start
  6.5 1.0 copy-done
  7.6 1.7 convolution_convert_fusion
  9.3 0.0 all-gather.2.cloned.1.call-update
  9.3 0.0 all-reduce.2.cloned.1.call-start
  9.4 76.0 %all-gather.2.cloned.1.call-done = bf16[4,1,512,512]{3,2,0,1:T(8,128)(2,1)} async-done(((bf16[4,1,16,512]{3,2,0,1:T(8,128)(2,1)}), bf16[4,1,512,512]{3,2,0,1:T(8,128)(2,1)}) %all-gather.2.cloned.1.call-update) | async-done | bytes 2097168 | tf_op jit(solution)/shard_map/all_gather | solution.py:22
  85.3 0.0 copy-start.2
  85.3 0.0 copy-start.3
  85.3 2.3 select_bitcast_fusion
  87.6 0.0 all-reduce.2.cloned.1.call-update
  87.7 115.9 %all-reduce.2.cloned.1.call-done = bf16[2,512,512]{2,1,0:T(8,128)(2,1)} async-done(((bf16[2,512,512]{2,1,0:T(8,128)(2,1)}), bf16[2,512,512]{2,1,0:T(8,128)(2,1)}) %all-reduce.2.cloned.1.call-update) | async-done | bytes 1048592 | tf_op jit(solution)/shard_map/psum | solution.py:9
  203.6 0.1 broadcast_in_dim.15
  203.6 0.0 copy-done.2
  203.6 0.0 copy-done.3
  203.7 18.1 %while.13 = (s32[]{:T(128)}, bf16[2,512,512]{2,1,0:T(8,128)(2,1)S(1)}, s32[]{:T(128)}, s32[2]{0:T(128)S(1)}, bf16[4,512,512]{2,1,0:T(8,128)(2,1)}, /*index=5*/s3...) while((s32[]{:T(128)}, ...), condition=%wide.region_2.3_spmd, body=%wide.region_1.2_spmd.sunk | while | flops 268959776 | bytes 1573451 | solution.py:47
  204.3 0.6 dynamic_slice.51
  207.5 0.6 dynamic_slice.50
  210.7 1.7 fusion.15
  213.1 0.6 dynamic_slice.51
  216.3 0.6 dynamic_slice.50
  219.5 1.7 fusion.15
  221.8 0.0 copy-start.1
  221.8 1.0 copy-done.1
Async XLA Ops:
  6.5 1.0 copy-start
  6.5 78.8 %all-gather.2.cloned.1.call-start = ((), (), s32[]{:S(2)}) async-start(), calls=%async_computation | async-start | bytes 2162688 | tf_op jit(solution)/shard_map/all_gather | solution.py:22
  9.3 194.3 %all-reduce.2.cloned.1.call-start = ((), (), s32[]{:S(2)}) async-start(), calls=%async_computation.1 | async-start | bytes 2097152 | tf_op jit(solution)/shard_map/psum | solution.py:9
  85.3 118.3 %copy-start.2 = (s32[1,1,2]{2,1,0:T(1,128)S(1)}, s32[1,1,2]{2,1,0:T(1,128)}, u32[]{:S(2)}) copy-start(s32[1,1,2]{2,1,0:T(1,128)} %param.9) | copy-start | bytes 28
  85.3 118.3 %copy-start.3 = (s32[1,1,2]{2,1,0:T(1,128)S(1)}, s32[1,1,2]{2,1,0:T(1,128)}, u32[]{:S(2)}) copy-start(s32[1,1,2]{2,1,0:T(1,128)} %param.10) | copy-start | bytes 28
  221.8 1.0 copy-start.1
Sparse Core Ops, SparseCore 0:
  9.5 75.7 all-gather.1
  88.6 114.9 all-reduce.1
where the time goes:
time: 230 us
  waiting for transfers between devices  192 us (83%)
  between operations  13.5 us (6%)
  loops' own time  12.4 us (5%)
  matrix products  5.03 us (2%)
  local copies, waits for them, and re-layouts  4.43 us (2%)
    psum x1, waiting for transfers between devices, broadcast(): return lax.psum(kept, axis)  116 us
    all_gather x1, waiting for transfers between devices, body(): lax.all_gather(solved, 'col', axis=2, tiled=True)  76 us
    another operation x1, loops' own time, body(): result = lax.fori_loop(0, live_here, update, result)  12.4 us
  transfers between devices with their start and end apart: 2, of which 2 were waited for; matrix products, arithmetic and copies ran while one was open for 0% of the time, Pallas kernels for 0%

commit v1 on v0

--- a/solution.py
+++ b/solution.py
@@ -19,9 +19,16 @@
         panel.reshape(-1, tile_width), inverse_factor, preferred_element_type=jnp.float32
     )
     solved = solved.astype(jnp.bfloat16).reshape(panel_count, 1, part_rows, tile_width)
-    row_blocks = lax.all_gather(solved, "col", axis=2, tiled=True).reshape(
-        panel_count, tile_width, tile_width
+    stocks_clear = lambda array_in, axis_id: jnp.concatenate(
+        lax.all_to_all(
+            jnp.stack([array_in for _ in range(lax.axis_size(axis_id))], axis=0),
+            axis_name=axis_id,
+            split_axis=0,
+            concat_axis=0,
+        ),
+        axis=2,
     )
+    row_blocks = stocks_clear(solved, "col").reshape(panel_count, tile_width, tile_width)
     position = lax.axis_index("col")
     grouped = row_blocks.reshape(column_count, col_ratio, tile_width, tile_width)
     picked = lax.dynamic_index_in_dim(grouped, position // grid_rows, 1, keepdims=False)

time: 230 us -> 265 us (1.15)
  waiting for transfers between devices: 192 us -> 210 us
  starting transfers between devices: 0.04 us -> 15.4 us
  local copies, waits for them, and re-layouts: 4.43 us -> 7.57 us
    all_to_all x0 -> x1, waiting for transfers between devices: none -> 100 us  [body(): lax.all_to_all(jnp.stack([array_in for _ in range(lax.axis_size(axis_id))...]
    all_gather x1 -> x0, waiting for transfers between devices: 76 us -> none  [body(): lax.all_gather(solved, 'col', axis=2, tiled=True)]
    all_to_all x0 -> x1, starting transfers between devices: none -> 15.4 us  [body(): lax.all_to_all(jnp.stack([array_in for _ in range(lax.axis_size(axis_id))...]
    psum x1, waiting for transfers between devices: 116 us -> 110 us  [broadcast(): return lax.psum(kept, axis)]
where the time goes in v1:
time: 265 us
  waiting for transfers between devices  210 us (79%)
  starting transfers between devices  15.4 us (6%)
  between operations  13.5 us (5%)
  loops' own time  12.4 us (5%)
  local copies, waits for them, and re-layouts  7.57 us (3%)
  matrix products  4.39 us (2%)
    psum x1, waiting for transfers between devices, broadcast(): return lax.psum(kept, axis)  110 us
    all_to_all x1, waiting for transfers between devices, body(): lax.all_to_all(jnp.stack([array_in for _ in range(lax.axis_size(axis_id))...  100 us
    all_to_all x1, starting transfers between devices, body(): lax.all_to_all(jnp.stack([array_in for _ in range(lax.axis_size(axis_id))...  15.4 us
    another operation x1, loops' own time, body(): result = lax.fori_loop(0, live_here, update, result)  12.4 us
  transfers between devices with their start and end apart: 2, of which 2 were waited for; matrix products, arithmetic and copies ran while one was open for 0% of the time, Pallas kernels for 0%

profile of v1, /device:TPU:32, one launch (start us, length us, event | category | flops | bytes accessed | tf_op | source)
XLA Modules:
  0.0 264.7 jit_solution(14646387160080373537)
XLA Ops:
  6.5 0.0 copy-start
  6.5 1.0 copy-done
  7.6 1.0 convolution_convert_fusion
  8.6 1.6 stack.3
  10.2 15.4 %all-to-all-start = ((bf16[32,4,1,16,512]{4,3,1,2,0:T(8,128)(2,1)}), bf16[32,4,1,16,512]{4,3,1,2,0:T(8,128)(2,1)S(1)}, u32[]{:S(2)}, u32[]{:S(2)}) async-start(bf16[32,4,1,16,512]{4,3,1,2,0:T(8,128)(2,1)} %stack.3), calls=%async_computation | async-start | bytes 4194304 | tf_op jit(solution)/shard_map/all_to_all | solution.py:23
  25.6 0.0 all-reduce.2.cloned.1.call-start
  25.7 100.1 %all-to-all-done = bf16[32,4,1,16,512]{4,3,1,2,0:T(8,128)(2,1)S(1)} async-done(((bf16[32,4,1,16,512]{4,3,1,2,0:T(8,128)(2,1)}), bf16[32,4,1,16,512]{4,3,1,2,0:T(8,128)(2,1)S(1)}, u32[]{:S(2)}, u32[]{:S(2)}) %all-to-all-start) | async-done | bytes 2097184 | tf_op jit(solution)/shard_map/all_to_all | solution.py:23
  125.7 0.2 copy.6
  125.9 0.0 copy-start.1
  125.9 1.3 copy-done.1
  127.3 0.0 copy-start.3
  127.3 0.0 copy-start.4
  127.3 1.0 select_bitcast_fusion
  128.3 0.0 all-reduce.2.cloned.1.call-update
  128.3 110.3 %all-reduce.2.cloned.1.call-done = bf16[2,512,512]{2,1,0:T(8,128)(2,1)} async-done(((bf16[2,512,512]{2,1,0:T(8,128)(2,1)}), bf16[2,512,512]{2,1,0:T(8,128)(2,1)}) %all-reduce.2.cloned.1.call-update) | async-done | bytes 1048592 | tf_op jit(solution)/shard_map/psum | solution.py:9
  238.7 0.1 broadcast_in_dim.15
  238.8 0.0 copy-done.3
  238.8 0.0 copy-done.4
  238.8 18.1 %while.13 = (s32[]{:T(128)}, bf16[2,512,512]{2,1,0:T(8,128)(2,1)S(1)}, s32[]{:T(128)}, s32[2]{0:T(128)S(1)}, bf16[4,512,512]{2,1,0:T(8,128)(2,1)}, /*index=5*/s3...) while((s32[]{:T(128)}, ...), condition=%wide.region_2.3_spmd, body=%wide.region_1.2_spmd.sunk | while | flops 268959776 | bytes 1573443 | solution.py:54
  239.5 0.6 dynamic_slice.51
  242.6 0.6 dynamic_slice.50
  245.8 1.7 fusion.15
  248.2 0.6 dynamic_slice.51
  251.4 0.6 dynamic_slice.50
  254.6 1.7 fusion.15
  256.9 0.0 copy-start.2
  256.9 1.0 copy-done.2
Async XLA Ops:
  6.5 1.0 copy-start
  10.2 115.5 %all-to-all-start = ((bf16[32,4,1,16,512]{4,3,1,2,0:T(8,128)(2,1)}), bf16[32,4,1,16,512]{4,3,1,2,0:T(8,128)(2,1)S(1)}, u32[]{:S(2)}, u32[]{:S(2)}) async-start(bf16[32,4,1,16,512]{4,3,1,2,0:T(8,128)(2,1)} %stack.3), calls=%async_computation | async-start | bytes 4194304 | tf_op jit(solution)/shard_map/all_to_all | solution.py:23
  25.6 213.1 %all-reduce.2.cloned.1.call-start = ((), (), s32[]{:S(2)}) async-start(), calls=%async_computation.1 | async-start | bytes 2097152 | tf_op jit(solution)/shard_map/psum | solution.py:9
  125.9 1.3 copy-start.1
  127.3 111.5 %copy-start.3 = (s32[1,1,2]{2,1,0:T(1,128)S(1)}, s32[1,1,2]{2,1,0:T(1,128)}, u32[]{:S(2)}) copy-start(s32[1,1,2]{2,1,0:T(1,128)} %param.9) | copy-start | bytes 28
  127.3 111.5 %copy-start.4 = (s32[1,1,2]{2,1,0:T(1,128)S(1)}, s32[1,1,2]{2,1,0:T(1,128)}, u32[]{:S(2)}) copy-start(s32[1,1,2]{2,1,0:T(1,128)} %param.10) | copy-start | bytes 28
  256.9 1.0 copy-start.2
Sparse Core Ops, SparseCore 0:
  128.5 110.1 all-reduce.1
